TPU v7x, 32 devices: a whole 2x2x4 slice. The times are simulated.
32 devices in a mesh: seq: 2 (over x), fsdp: 16 (over z, y, core).
Axes of the slice: x: 2, y: 2, z: 4, core: 2. Of those that a mesh axis runs over, the one named last changes fastest.
Arguments:
- tokens: bfloat16 [4096, 1024], P(('fsdp', 'seq')), may hold values from -6 to 6
- cotangent: bfloat16 [4096, 1024], P(('fsdp', 'seq')), may hold values from -6 to 6
- documents: int32 [16, 256], P('fsdp'), may hold values from 0 to 3, never falling along the last dimension, each value on 1 to 128 neighbouring positions
- in_weight: bfloat16 [1024, 4384], P('fsdp'), may hold values from -0.1875 to 0.1875
- kernel_taps: float32 [4, 2304], replicated, may hold values from -3 to 3
- kernel_bias: float32 [2304], replicated, may hold values from -0.5 to 0.5
- step_bias: float32 [32], replicated, may hold values from -6 to -2
- decay_log: float32 [32], replicated, may hold values from 0 to 2.77
- skip_gain: float32 [32], replicated, may hold values from 0.5 to 1.5
- pre_gain: float32 [1024], replicated, may hold values from 0.5 to 1.5
- norm_gain: float32 [2048], replicated, may hold values from 0.5 to 1.5
- out_weight: bfloat16 [2048, 1024], P('fsdp'), may hold values from -0.125 to 0.125
Outputs:
- block_output: bfloat16 [4096, 1024], P(('fsdp', 'seq'))
- tokens_grad: float32 [4096, 1024], P(('fsdp', 'seq'))
- in_weight_grad: float32 [1024, 4384], P('fsdp')
- kernel_taps_grad: float32 [4, 2304], replicated
- kernel_bias_grad: float32 [2304], replicated
- step_bias_grad: float32 [32], replicated
- decay_log_grad: float32 [32], replicated
- skip_gain_grad: float32 [32], replicated
- pre_gain_grad: float32 [1024], replicated
- norm_gain_grad: float32 [2048], replicated
- out_weight_grad: float32 [2048, 1024], P('fsdp')
Inputs may be any that keep to these rules, and one draw needn't show every extreme that they name: `documents`: in every sequence the ids start at 0 and never fall; each id marks one document of consecutive tokens, and every id of 0 to 3 occurs.
All inputs are finite; a program needn't handle non-finite values.
Results may differ from a plain program's by a relative error of at most 0.011.
Values may be sent and summed in bfloat16 or wider, within the bound.
A program may use at most 128 MiB of HBM per device.

v0:
```python
from functools import partial
import jax
import jax.numpy as jnp
from jax import lax
from jax.sharding import PartitionSpec as P

HEADS = 32
HEAD_DIM = 64
STATE = 128
CONV = 4
SPAN = 256
INNER = 2048
CONV_CH = 2304
norm_epsilon = 1e-05


def pre_norm(values, gain):
    scale = lax.rsqrt(jnp.mean(values * values, axis=-1, keepdims=True) + norm_epsilon)
    return values * scale * gain


def gate_norm(mixed, gates, gain):
    gated = mixed * jax.nn.silu(gates)
    scale = lax.rsqrt(jnp.mean(gated * gated, axis=-1, keepdims=True) + norm_epsilon)
    return gated * scale * gain


def block_step(state, block):
    scaled, input_matrix, output_matrix, log_block, seg_block, prev_last = block
    width = seg_block.shape[0]
    cumul = jnp.cumsum(log_block, axis=0).T
    places = jnp.arange(width)
    causal = (places[:, None] >= places[None, :]) & (seg_block[:, None] == seg_block[None, :])
    log_gap = cumul[:, :, None] - cumul[:, None, :]
    decay = jnp.where(causal[None], jnp.exp(jnp.where(causal[None], log_gap, 0.0)), 0.0)
    scores = jnp.dot(output_matrix, input_matrix.T, precision=lax.Precision.HIGHEST)
    inside = jnp.einsum(
        "hij,jhp->ihp", decay * scores[None], scaled, precision=lax.Precision.HIGHEST
    )
    entering = jnp.exp(cumul) * (seg_block == prev_last).astype(jnp.float32)[None]
    carried = (
        jnp.einsum("in,hnp->ihp", output_matrix, state, precision=lax.Precision.HIGHEST)
        * entering.T[:, :, None]
    )
    final = cumul[:, -1]
    leaving = (
        jnp.exp(final[:, None] - cumul) * (seg_block == seg_block[-1]).astype(jnp.float32)[None]
    )
    fresh = jnp.einsum(
        "hj,jn,jhp->hnp", leaving, input_matrix, scaled, precision=lax.Precision.HIGHEST
    )
    keeping = jnp.exp(final) * (seg_block[-1] == prev_last).astype(jnp.float32)
    new_state = keeping[:, None, None] * state + fresh
    return (new_state, inside + carried)


def mixer(segment, conv_in, step_raw, taps, tap_bias, bias_steps, log_rates, skips):
    length, channels = conv_in.shape
    heads = step_raw.shape[1]
    width = heads * HEAD_DIM
    summed = tap_bias + conv_in * taps[CONV - 1]
    for offset in range(1, CONV):
        shifted = jnp.concatenate(
            [jnp.zeros((offset, channels), jnp.float32), conv_in[: length - offset]], axis=0
        )
        matched = jnp.concatenate(
            [
                jnp.zeros((offset,), jnp.float32),
                (segment[offset:] == segment[: length - offset]).astype(jnp.float32),
            ]
        )
        summed = summed + taps[CONV - 1 - offset] * shifted * matched[:, None]
    active = jax.nn.silu(summed)
    values = active[:, :width].reshape(length, heads, HEAD_DIM)
    input_matrix = active[:, width : width + STATE]
    output_matrix = active[:, width + STATE :]
    steps_taken = jax.nn.softplus(step_raw + bias_steps)
    log_decay = steps_taken * -jnp.exp(log_rates)
    scaled = values * steps_taken[:, :, None]
    blocks = length // SPAN
    seg_blocks = segment.reshape(blocks, SPAN)
    prev_last = jnp.concatenate([seg_blocks[:1, 0], seg_blocks[:-1, -1]])
    initial = jnp.zeros((heads, STATE, HEAD_DIM), jnp.float32)
    _, outputs = lax.scan(
        block_step,
        initial,
        (
            scaled.reshape(blocks, SPAN, heads, HEAD_DIM),
            input_matrix.reshape(blocks, SPAN, STATE),
            output_matrix.reshape(blocks, SPAN, STATE),
            log_decay.reshape(blocks, SPAN, heads),
            seg_blocks,
            prev_last,
        ),
    )
    result = outputs.reshape(length, heads, HEAD_DIM) + values * skips[None, :, None]
    return result.reshape(length, width)


def local(
    tokens,
    cotangent,
    documents,
    in_weight,
    kernel_taps,
    kernel_bias,
    step_bias,
    decay_log,
    skip_gain,
    pre_gain,
    norm_gain,
    out_weight,
):
    group_count = lax.axis_size("seq")
    group_index = lax.axis_index("seq")
    local_heads = HEADS // group_count
    local_width = local_heads * HEAD_DIM
    head_start = group_index * local_width
    head_first = group_index * local_heads
    contract_rows = (((1,), (1,)), ((), ()))
    contract_tokens = (((0,), (0,)), ((), ()))
    floats = tokens.astype(jnp.float32)
    normed_in = pre_norm(floats, pre_gain).astype(jnp.bfloat16)
    in_whole = lax.all_gather(in_weight, "fsdp", axis=0, tiled=True)
    projected = jnp.dot(normed_in, in_whole, preferred_element_type=jnp.float32).astype(
        jnp.bfloat16
    )
    gates = projected[:, :INNER]
    values_raw = projected[:, INNER : 2 * INNER]
    state_raw = projected[:, 2 * INNER : INNER + CONV_CH]
    step_raw = projected[:, INNER + CONV_CH :]
    head_values, head_steps = (
        lax.all_to_all(values_raw, "seq", split_axis=1, concat_axis=0, tiled=True),
        lax.all_to_all(step_raw, "seq", split_axis=1, concat_axis=0, tiled=True),
    )
    state_whole = lax.all_gather(state_raw, "seq", axis=0, tiled=True)
    segment = documents[0]
    local_taps = jnp.concatenate(
        [lax.dynamic_slice_in_dim(kernel_taps, head_start, local_width, 1), kernel_taps[:, INNER:]],
        axis=1,
    )
    local_bias = jnp.concatenate(
        [lax.dynamic_slice_in_dim(kernel_bias, head_start, local_width, 0), kernel_bias[INNER:]],
        axis=0,
    )
    local_step_bias = lax.dynamic_slice_in_dim(step_bias, head_first, local_heads, 0)
    local_decay = lax.dynamic_slice_in_dim(decay_log, head_first, local_heads, 0)
    local_skip = lax.dynamic_slice_in_dim(skip_gain, head_first, local_heads, 0)
    conv_in = jnp.concatenate(
        [head_values.astype(jnp.float32), state_whole.astype(jnp.float32)], axis=1
    )
    mixed, mixer_back = jax.vjp(
        partial(mixer, segment),
        conv_in,
        head_steps.astype(jnp.float32),
        local_taps,
        local_bias,
        local_step_bias,
        local_decay,
        local_skip,
    )
    token_mixed = lax.all_to_all(
        mixed.astype(jnp.bfloat16), "seq", split_axis=0, concat_axis=1, tiled=True
    )
    normed_out, norm_back = jax.vjp(
        gate_norm, token_mixed.astype(jnp.float32), gates.astype(jnp.float32), norm_gain
    )
    normed_bf = normed_out.astype(jnp.bfloat16)
    out_whole = lax.all_gather(out_weight, "fsdp", axis=0, tiled=True)
    branch = jnp.dot(normed_bf, out_whole, preferred_element_type=jnp.float32)
    block_output = (floats + branch).astype(jnp.bfloat16)
    back_normed = lax.dot_general(
        cotangent, out_whole, contract_rows, preferred_element_type=jnp.float32
    )
    columns = normed_bf
    outward_grad = lax.psum_scatter(
        lax.dot_general(columns, cotangent, contract_tokens, preferred_element_type=jnp.float32),
        "fsdp",
        scatter_dimension=0,
        tiled=True,
    )
    back_mixed, back_gates, norm_gain_part = norm_back(back_normed)
    head_back = lax.all_to_all(
        back_mixed.astype(jnp.bfloat16), "seq", split_axis=1, concat_axis=0, tiled=True
    )
    back_conv, back_steps, taps_part, bias_part, step_part, decay_part, skip_part = mixer_back(
        head_back.astype(jnp.float32)
    )
    back_values, back_step_tokens = (
        lax.all_to_all(
            back_conv[:, :local_width].astype(jnp.bfloat16),
            "seq",
            split_axis=0,
            concat_axis=1,
            tiled=True,
        ),
        lax.all_to_all(
            back_steps.astype(jnp.bfloat16), "seq", split_axis=0, concat_axis=1, tiled=True
        ),
    )
    back_state = lax.psum_scatter(
        back_conv[:, local_width:].astype(jnp.bfloat16), "seq", scatter_dimension=0, tiled=True
    )
    back_projected = jnp.concatenate(
        [back_gates.astype(jnp.bfloat16), back_values, back_state, back_step_tokens], axis=1
    )
    back_normed_in = lax.dot_general(
        back_projected, in_whole, contract_rows, preferred_element_type=jnp.float32
    )
    columns = normed_in
    inward_grad = lax.psum_scatter(
        lax.dot_general(
            columns, back_projected, contract_tokens, preferred_element_type=jnp.float32
        ),
        "fsdp",
        scatter_dimension=0,
        tiled=True,
    )
    inward_grad, outward_grad = lax.psum((inward_grad, outward_grad), "seq")
    _, pre_back = jax.vjp(pre_norm, floats, pre_gain)
    back_floats, pre_gain_part = pre_back(back_normed_in)
    tokens_grad = cotangent.astype(jnp.float32) + back_floats
    taps_full = lax.dynamic_update_slice_in_dim(
        jnp.zeros_like(kernel_taps), taps_part[:, :local_width], head_start, 1
    )
    taps_full = taps_full.at[:, INNER:].set(taps_part[:, local_width:])
    bias_full = lax.dynamic_update_slice_in_dim(
        jnp.zeros_like(kernel_bias), bias_part[:local_width], head_start, 0
    )
    bias_full = bias_full.at[INNER:].set(bias_part[local_width:])
    step_full = lax.dynamic_update_slice_in_dim(jnp.zeros_like(step_bias), step_part, head_first, 0)
    decay_full = lax.dynamic_update_slice_in_dim(
        jnp.zeros_like(decay_log), decay_part, head_first, 0
    )
    skip_full = lax.dynamic_update_slice_in_dim(jnp.zeros_like(skip_gain), skip_part, head_first, 0)
    totals = lax.psum(
        (taps_full, bias_full, step_full, decay_full, skip_full, pre_gain_part, norm_gain_part),
        ("seq", "fsdp"),
    )
    return (
        block_output,
        tokens_grad,
        inward_grad,
        totals[0],
        totals[1],
        totals[2],
        totals[3],
        totals[4],
        totals[5],
        totals[6],
        outward_grad,
    )


def solution(mesh):
    return jax.shard_map(
        local,
        mesh=mesh,
        in_specs=(
            P(("fsdp", "seq"), None),
            P(("fsdp", "seq"), None),
            P("fsdp", None),
            P("fsdp", None),
            P(),
            P(),
            P(),
            P(),
            P(),
            P(),
            P(),
            P("fsdp", None),
        ),
        out_specs=(
            P(("fsdp", "seq"), None),
            P(("fsdp", "seq"), None),
            P("fsdp", None),
            P(),
            P(),
            P(),
            P(),
            P(),
            P(),
            P(),
            P("fsdp", None),
        ),
        check_vma=False,
    )
```

profile of v0, /device:TPU:0, one launch (start us, length us, event | category | flops | bytes accessed | tf_op | source)
XLA Modules:
  0.0 587.1 jit_solution(15330456754907170330)
XLA Ops:
  20.2 2.6 compare_convert_fusion
  24.2 68.1 %all-gather.3.cloned.1.call-done = bf16[1024,4384]{1,0:T(8,128)(2,1)} async-done(((bf16[64,4384]{1,0:T(8,128)(2,1)}), bf16[1024,4384]{1,0:T(8,128)(2,1)}) %all-gather.3.cloned.1.call-update) | async-done | bytes 8978448 | tf_op jit(solution)/shard_map/all_gather | solution.py:124
  92.3 7.3 %convolution_convert_fusion = bf16[128,4384]{0,1:T(8,128)(2,1)S(1)} fusion(bf16[1024,4384]{1,0:T(8,128)(2,1)} %all-gather.3.cloned.1.call-done, bf16[128,1024]{1,0:T(8,128)(2,1)S(1)} %copy-done.4, f32[1024]{0:T(1024)S(1)} %copy-done.23, f32[128]{0:T(128)S(1)} %fusion.99), kind=kOutput, calls=%fused_computation | convolution fusion | flops 1150324736 | bytes 10367488 | tf_op jit(solution)/shard_map/dot_general | solution.py:125
  100.3 3.2 all-to-all-start
  103.6 5.0 all_gather.10
  109.5 3.8 all-to-all-start.1
  115.6 5.5 all-to-all-done.1
  125.3 2.9 multiply_reduce_fusion.5
  133.0 6.2 %fusion.27 = f32[256,16,64]{0,2,1:T(8,128)} fusion(f32[256,256]{1,0:T(8,128)S(1)} %fusion.73, f32[16,256]{1,0:T(8,128)S(1)} %copy-done.44, pred[256,256]{1,0:T(8,128)(4,1)S(1)} %copy-done.47, f32[256,16,64]{0,2,1:T(8,128)S(1)} %bitcast.205, f32[256,16,64]{0,2,1:T(8,128)S(1)} %bitcast.193, f32[256,16]{0,1:T(8,128)S(1)} %get-tuple-element.355, ...), kind=kOutput, calls=%fused_computation.29 | convolution fusion | flops 810287104 | bytes 3522560 | tf_op jit(solution)/shard_map/jvp()/while/body/eval_jaxpr/hij,jhp->ihp/dot_general | solution.py:37
  144.3 9.4 %all_to_all.93 = bf16[2,128,1024]{1,2,0:T(8,128)(2,1)S(1)} all-to-all(bf16[2,128,1024]{1,2,0:T(8,128)(2,1)S(1)} %copy.127), channel_id=1, replica_groups=mesh['seq'=2,'fsdp'=16] {'seq'}, dimensions={0} | all-to-all | bytes 1048576 | tf_op jit(solution)/shard_map/all_to_all | solution.py:162
  156.9 4.2 multiply_reduce_fusion.6
  161.2 2.8 fusion.41
  164.0 4.2 all-to-all-start.3
  170.6 2.7 mul.647
  173.3 3.2 convolution_bitcast_fusion
  181.1 5.8 fusion.7
  186.9 4.8 fusion.34
  191.7 2.7 copy.132
  198.1 3.2 convolution_bitcast_fusion.1
  210.0 4.6 fusion.110
  215.6 2.5 reduce-window.28
  219.0 3.2 all-to-all-start.5
  223.4 2.7 all-to-all-done.5
  226.1 3.5 all-to-all-start.4
  230.6 5.5 all-to-all-done.4
  236.2 9.2 %fusion.68 = f32[1024,4384]{1,0:T(8,128)} fusion(bf16[128,32]{0,1:T(8,128)(2,1)S(1)} %bitcast.211, bf16[128,256]{0,1:T(8,128)(2,1)S(1)} %copy.149, bf16[128,2048]{0,1:T(8,128)(2,1)S(1)} %bitcast.199, bf16[128,2048]{0,1:T(8,128)(2,1)S(1)} %copy-done.13, bf16[128,1024]{1,0:T(8,128)(2,1)S(1)} %copy-done.5, f32[1024]{0:T(1024)S(1)} %copy-done.24, ...), kind=kOutput, calls=%fused_computation.108 | convolution fusion | flops 1154252800 | bytes 19345920 | tf_op jit(solution)/shard_map/dot_general | solution.py:212
  245.5 4.2 fusion.33
  253.8 73.3 %reduce-scatter.8.cloned.1.call-done = f32[128,1024]{1,0:T(8,128)} async-done(((f32[2048,1024]{1,0:T(8,128)}), f32[128,1024]{1,0:T(8,128)}) %reduce-scatter.8.cloned.1.call-update) | async-done | bytes 524304 | tf_op jit(solution)/shard_map/reduce_scatter | solution.py:176
  327.0 193.4 %reduce-scatter.6.cloned.1.call-done = f32[64,4384]{1,0:T(8,128)} async-done(((f32[1024,4384]{1,0:T(8,128)}), f32[64,4384]{1,0:T(8,128)}) %reduce-scatter.6.cloned.1.call-update) | async-done | bytes 1122320 | tf_op jit(solution)/shard_map/reduce_scatter | solution.py:211
  521.7 6.8 %fusion.51 = (f32[1024]{0:T(1024)S(1)}, f32[128]{0:T(128)S(1)}, f32[128,1024]{1,0:T(8,128)S(1)}) fusion(bf16[128,1024]{1,0:T(8,128)(2,1)S(1)} %copy-done.5, f32[128]{0:T(128)S(1)} %copy-done.59, f32[1024]{0:T(1024)S(1)} %copy-done.24, bf16[1024,4384]{1,0:T(8,128)(2,1)} %all-gather.3.cloned.1.call-done, bf16[128,32]{0,1:T(8,128)(2,1)S(1)} %bitcast.212, ...), kind=kOutput, calls=%fused_computation.90 | convolution fusion | flops 1154644864 | bytes 10896384 | tf_op jit(solution)/shard_map/dot_general | solution.py:207
  528.5 41.8 %all-reduce.16 = (f32[4,2304]{1,0:T(4,128)}, f32[2304]{0:T(1024)}, f32[32]{0:T(128)}, f32[32]{0:T(128)}, f32[32]{0:T(128)}, /*index=5*/f32[1024]{0:T(1024)}, f32[2048]{0:T(1024)}) all-reduce(f32[4,2304]{1,0:T(4,128)S(1)} %add_dynamic-update-slice_fusion, ...), channel_id=1, replica_groups=mesh['seq'=2,'fsdp'=16] {'seq','fsdp'}, use_global_device_ids=true, to_apply=%region_21.22 | all-reduce | flops 14688 | bytes 117504 | tf_op jit(solution)/shard_map/psum | solution.py:236
  571.3 5.5 all-reduce.20.cloned.1.call-done
  (288 shorter events, 67.7 us)
Async XLA Ops:
  7.2 85.1 %copy-start.4 = (bf16[128,1024]{1,0:T(8,128)(2,1)S(1)}, bf16[128,1024]{1,0:T(8,128)(2,1)}, u32[]{:S(2)}) copy-start(bf16[128,1024]{1,0:T(8,128)(2,1)} %param.16) | copy-start | bytes 786436
  7.2 85.1 %copy-start.23 = (f32[1024]{0:T(1024)S(1)}, f32[1024]{0:T(1024)}, u32[]{:S(2)}) copy-start(f32[1024]{0:T(1024)} %param.25) | copy-start | bytes 12292
  7.2 85.1 %all-gather.3.cloned.1.call-start = ((), (), s32[]{:S(2)}) async-start(), calls=%async_computation.9 | async-start | bytes 9748480 | tf_op jit(solution)/shard_map/all_gather | solution.py:124
  7.9 148.9 %all-gather.5.cloned.1.call-start = ((), (), s32[]{:S(2)}) async-start(), calls=%async_computation.10 | async-start | bytes 4456448 | tf_op jit(solution)/shard_map/all_gather | solution.py:169
  11.6 101.8 %copy-start.74 = (f32[16]{0:T(128)}, f32[16]{0:T(128)S(1)}, u32[]{:S(2)}) copy-start(f32[16]{0:T(128)S(1)} %dynamic_slice.89) | copy-start | bytes 196
  14.3 107.2 %copy-start.31 = (f32[1280]{0:T(1024)}, f32[1280]{0:T(1024)S(1)}, u32[]{:S(2)}) copy-start(f32[1280]{0:T(1024)S(1)} %get-tuple-element.316) | copy-start | bytes 15364
  14.3 107.2 %copy-start.33 = (f32[1280]{0:T(1024)}, f32[1280]{0:T(1024)S(1)}, u32[]{:S(2)}) copy-start(f32[1280]{0:T(1024)S(1)} %get-tuple-element.318) | copy-start | bytes 15364
  14.3 107.2 %copy-start.35 = (f32[1280]{0:T(1024)}, f32[1280]{0:T(1024)S(1)}, u32[]{:S(2)}) copy-start(f32[1280]{0:T(1024)S(1)} %get-tuple-element.319) | copy-start | bytes 15364
  14.3 107.2 %copy-start.37 = (f32[1280]{0:T(1024)}, f32[1280]{0:T(1024)S(1)}, u32[]{:S(2)}) copy-start(f32[1280]{0:T(1024)S(1)} %get-tuple-element.317) | copy-start | bytes 15364
  15.1 98.3 %copy-start.76 = (f32[16]{0:T(128)}, f32[16]{0:T(128)S(1)}, u32[]{:S(2)}) copy-start(f32[16]{0:T(128)S(1)} %fusion.100) | copy-start | bytes 196
  16.0 105.5 %copy-start.72 = (f32[256]{0:T(256)}, f32[256]{0:T(256)S(1)}, u32[]{:S(2)}) copy-start(f32[256]{0:T(256)S(1)} %pad_convert_fusion.1) | copy-start | bytes 3076
  17.8 103.8 %copy-start.66 = (f32[256]{0:T(256)}, f32[256]{0:T(256)S(1)}, u32[]{:S(2)}) copy-start(f32[256]{0:T(256)S(1)} %get-tuple-element.364) | copy-start | bytes 3076
  17.8 103.8 %copy-start.68 = (f32[256]{0:T(256)}, f32[256]{0:T(256)S(1)}, u32[]{:S(2)}) copy-start(f32[256]{0:T(256)S(1)} %get-tuple-element.365) | copy-start | bytes 3076
  20.2 79.5 %copy-start.79 = (f32[128]{0:T(128)}, f32[128]{0:T(128)S(1)}, u32[]{:S(2)}) copy-start(f32[128]{0:T(128)S(1)} %fusion.53) | copy-start | bytes 1540
  20.2 79.4 %copy-start.58 = (f32[128]{0:T(128)}, f32[128]{0:T(128)S(1)}, u32[]{:S(2)}) copy-start(f32[128]{0:T(128)S(1)} %fusion.99) | copy-start | bytes 1540
  100.3 9.2 %all-to-all-start = ((bf16[128,2,16]{0,2,1:T(8,128)(2,1)}), bf16[128,2,16]{0,2,1:T(8,128)(2,1)S(1)}, u32[]{:S(2)}, u32[]{:S(2)}) async-start(bf16[128,2,16]{0,2,1:T(8,128)(2,1)} %bitcast.3), calls=%async_computation | async-start | bytes 16384 | tf_op jit(solution)/shard_map/all_to_all | solution.py:134
  109.5 11.6 %all-to-all-start.1 = ((bf16[128,2,1024]{0,2,1:T(8,128)(2,1)}), bf16[128,2,1024]{0,2,1:T(8,128)(2,1)S(1)}, u32[]{:S(2)}, u32[]{:S(2)}) async-start(bf16[128,2,1024]{0,2,1:T(8,128)(2,1)} %bitcast.6), calls=%async_computation.1 | async-start | bytes 1048576 | tf_op jit(solution)/shard_map/all_to_all | solution.py:133
  164.0 12.5 %all-to-all-start.3 = ((bf16[128,2,1024]{0,2,1:T(8,128)(2,1)}), bf16[128,2,1024]{0,2,1:T(8,128)(2,1)}, u32[]{:S(2)}, u32[]{:S(2)}) async-start(bf16[128,2,1024]{0,2,1:T(8,128)(2,1)} %bitcast.201), calls=%async_computation.3 | async-start | bytes 1048576 | tf_op jit(solution)/shard_map/all_to_all | solution.py:183
  168.2 61.5 %reduce-scatter.10.cloned.1.call-start = ((), (), s32[]{:S(2)}) async-start(), calls=%async_computation.13 | async-start | bytes 196608
  209.9 117.1 %reduce-scatter.8.cloned.1.call-start = ((), (), s32[]{:S(2)}) async-start(), calls=%async_computation.12 | async-start | bytes 8912896 | tf_op jit(solution)/shard_map/reduce_scatter | solution.py:176
  219.0 7.0 %all-to-all-start.5 = ((bf16[2,128,16]{1,2,0:T(8,128)(2,1)}), bf16[2,128,16]{1,2,0:T(8,128)(2,1)S(1)}, u32[]{:S(2)}, u32[]{:S(2)}) async-start(bf16[2,128,16]{1,2,0:T(8,128)(2,1)} %copy_bitcast_fusion.3), calls=%async_computation.5 | async-start | bytes 16384 | tf_op jit(solution)/shard_map/all_to_all | solution.py:197
  222.3 13.8 %copy-start.5 = (bf16[128,1024]{1,0:T(8,128)(2,1)S(1)}, bf16[128,1024]{1,0:T(8,128)(2,1)}, u32[]{:S(2)}) copy-start(bf16[128,1024]{1,0:T(8,128)(2,1)} %param.16) | copy-start | bytes 786436
  222.3 13.8 %copy-start.13 = (bf16[128,2048]{0,1:T(8,128)(2,1)S(1)}, bf16[128,2048]{0,1:T(8,128)(2,1)}, u32[]{:S(2)}) copy-start(bf16[128,2048]{0,1:T(8,128)(2,1)} %get-tuple-element.342) | copy-start | bytes 1572868
  222.4 13.8 %copy-start.24 = (f32[1024]{0:T(1024)S(1)}, f32[1024]{0:T(1024)}, u32[]{:S(2)}) copy-start(f32[1024]{0:T(1024)} %param.25) | copy-start | bytes 12292
  222.4 13.8 %copy-start.59 = (f32[128]{0:T(128)S(1)}, f32[128]{0:T(128)}, u32[]{:S(2)}) copy-start(f32[128]{0:T(128)} %copy-done.58) | copy-start | bytes 1540
  226.1 10.1 %all-to-all-start.4 = ((bf16[2,128,1024]{1,2,0:T(8,128)(2,1)}), bf16[2,128,1024]{1,2,0:T(8,128)(2,1)S(1)}, u32[]{:S(2)}, u32[]{:S(2)}) async-start(bf16[2,128,1024]{1,2,0:T(8,128)(2,1)} %copy.133), calls=%async_computation.4 | async-start | bytes 1048576 | tf_op jit(solution)/shard_map/all_to_all | solution.py:190
  229.6 290.9 %reduce-scatter.6.cloned.1.call-start = ((), (), s32[]{:S(2)}) async-start(), calls=%async_computation.11 | async-start | bytes 19496960 | tf_op jit(solution)/shard_map/reduce_scatter | solution.py:211
  245.5 331.4 %all-reduce.20.cloned.1.call-start = ((), (), s32[]{:S(2)}) async-start(), calls=%async_computation.14 | async-start | bytes 3342336 | tf_op jit(solution)/shard_map/psum | solution.py:219
  253.7 266.8 %copy-start.49 = (f32[1280]{0:T(1024)S(1)}, f32[1280]{0:T(1024)}, u32[]{:S(2)}) copy-start(f32[1280]{0:T(1024)} %get-tuple-element.312) | copy-start | bytes 15364
  253.7 267.8 %copy-start.85 = (f32[32]{0:T(128)S(1)}, f32[32]{0:T(128)}, u32[]{:S(2)}) copy-start(f32[32]{0:T(128)} %param.23) | copy-start | bytes 388
  253.7 267.9 %copy-start.15 = (bf16[2,128,1024]{1,2,0:T(8,128)(2,1)S(1)}, bf16[2,128,1024]{1,2,0:T(8,128)(2,1)}, u32[]{:S(2)}) copy-start(bf16[2,128,1024]{1,2,0:T(8,128)(2,1)} %copy-done.14) | copy-start | bytes 1572868
  521.6 48.7 %copy-start.80 = (f32[128]{0:T(128)S(1)}, f32[128]{0:T(128)}, u32[]{:S(2)}) copy-start(f32[128]{0:T(128)} %copy-done.79) | copy-start | bytes 1540
  (65 other events, 235.5 us)
Sparse Core Ops, SparseCore 0:
  10.3 81.9 all-gather.2
  94.5 48.8 all-gather.4
  210.0 9.5 reduce-scatter.9
  223.5 103.4 reduce-scatter.7
  331.1 189.3 reduce-scatter.5
  522.7 54.1 all-reduce.19
where the time goes:
time: 593 us; the launch traced here: 587 us
  waiting for transfers between devices  356 us (60%)
  matrix products  68.8 us (12%)
  blocking collectives  56.2 us (9%)
  local copies, waits for them, and re-layouts  41.7 us (7%)
  other arithmetic  30.7 us (5%)
  starting transfers between devices  18.7 us (3%)
  between operations  15.5 us (3%)
    reduce_scatter x1, waiting for transfers between devices, local(): lax.psum_scatter(lax.dot_general(columns, back_projected, contract_tokens...  193 us
    reduce_scatter x1, waiting for transfers between devices, local(): lax.psum_scatter(lax.dot_general(columns, cotangent, contract_tokens, pre...  73.3 us
    all_gather x1, waiting for transfers between devices, local(): in_whole = lax.all_gather(in_weight, 'fsdp', axis=0, tiled=True)  68.1 us
    psum x1, blocking collectives, local(): lax.psum((taps_full, bias_full, step_full, decay_full, skip_full, pre_gai...  41.8 us
    dot_general x3, matrix products, block_step(): jnp.einsum('hij,jhp->ihp', decay * scores[None], scaled, precision=lax.Pr...  16.8 us
  transfers between devices with their start and end apart: 11, of which 7 were waited for; matrix products, arithmetic and copies ran while one was open for 16% of the time, Pallas kernels for 0%

commit v1 on v0

--- a/solution.py
+++ b/solution.py
@@ -234,8 +234,11 @@
     )
     skip_full = lax.dynamic_update_slice_in_dim(jnp.zeros_like(skip_gain), skip_part, head_first, 0)
     totals = lax.psum(
-        (taps_full, bias_full, step_full, decay_full, skip_full, pre_gain_part, norm_gain_part),
-        ("seq", "fsdp"),
+        lax.psum(
+            (taps_full, bias_full, step_full, decay_full, skip_full, pre_gain_part, norm_gain_part),
+            "fsdp",
+        ),
+        "seq",
     )
     return (
         block_output,

time: 593 us -> 615 us (1.037)
  blocking collectives: 56.2 us -> 83.4 us
  waiting for transfers between devices: 356 us -> 349 us
    psum x1, blocking collectives: 41.8 us -> 59.6 us  [local(): lax.psum((taps_full, bias_full, step_full, decay_full, skip_full, pre_gai...]
    psum x0 -> x1, blocking collectives: none -> 9.36 us  [local(): lax.psum(lax.psum((taps_full, bias_full, step_full, decay_full, skip_full...]
  transfers between devices with their start and end apart: 11 -> 11, of which waited for: 7 -> 6; matrix products, arithmetic and copies ran while one was open for 16% -> 16% of each run, Pallas kernels for 0% -> 0%
where the time goes in v1:
time: 615 us; the launch traced here: 609 us
  waiting for transfers between devices  349 us (57%)
  blocking collectives  83.4 us (14%)
  matrix products  68.7 us (11%)
  local copies, waits for them, and re-layouts  42.8 us (7%)
  other arithmetic  31.4 us (5%)
  starting transfers between devices  18.7 us (3%)
  between operations  15.5 us (3%)
    reduce_scatter x1, waiting for transfers between devices, local(): lax.psum_scatter(lax.dot_general(columns, back_projected, contract_tokens...  193 us
    reduce_scatter x1, waiting for transfers between devices, local(): lax.psum_scatter(lax.dot_general(columns, cotangent, contract_tokens, pre...  71.8 us
    all_gather x1, waiting for transfers between devices, local(): in_whole = lax.all_gather(in_weight, 'fsdp', axis=0, tiled=True)  68.1 us
    psum x1, blocking collectives, local(): lax.psum((taps_full, bias_full, step_full, decay_full, skip_full, pre_gai...  59.6 us
    dot_general x3, matrix products, block_step(): jnp.einsum('hij,jhp->ihp', decay * scores[None], scaled, precision=lax.Pr...  16.7 us
  transfers between devices with their start and end apart: 11, of which 6 were waited for; matrix products, arithmetic and copies ran while one was open for 16% of the time, Pallas kernels for 0%

profile of v1, /device:TPU:0, one launch (start us, length us, event | category | flops | bytes accessed | tf_op | source)
XLA Modules:
  0.0 609.0 jit_solution(440748634658551265)
XLA Ops:
  20.2 2.6 compare_convert_fusion
  24.2 68.1 %all-gather.3.cloned.1.call-done = bf16[1024,4384]{1,0:T(8,128)(2,1)} async-done(((bf16[64,4384]{1,0:T(8,128)(2,1)}), bf16[1024,4384]{1,0:T(8,128)(2,1)}) %all-gather.3.cloned.1.call-update) | async-done | bytes 8978448 | tf_op jit(solution)/shard_map/all_gather | solution.py:124
  92.3 7.3 %convolution_convert_fusion = bf16[128,4384]{0,1:T(8,128)(2,1)S(1)} fusion(bf16[1024,4384]{1,0:T(8,128)(2,1)} %all-gather.3.cloned.1.call-done, bf16[128,1024]{1,0:T(8,128)(2,1)S(1)} %copy-done.4, f32[1024]{0:T(1024)S(1)} %copy-done.23, f32[128]{0:T(128)S(1)} %fusion.99), kind=kOutput, calls=%fused_computation | convolution fusion | flops 1150324736 | bytes 10367488 | tf_op jit(solution)/shard_map/dot_general | solution.py:125
  100.3 3.2 all-to-all-start
  103.6 5.0 all_gather.10
  109.5 3.8 all-to-all-start.1
  115.6 5.5 all-to-all-done.1
  125.3 2.9 multiply_reduce_fusion.5
  133.0 6.2 %fusion.27 = f32[256,16,64]{0,2,1:T(8,128)} fusion(f32[256,256]{1,0:T(8,128)S(1)} %fusion.73, f32[16,256]{1,0:T(8,128)S(1)} %copy-done.44, pred[256,256]{1,0:T(8,128)(4,1)S(1)} %copy-done.47, f32[256,16,64]{0,2,1:T(8,128)S(1)} %bitcast.205, f32[256,16,64]{0,2,1:T(8,128)S(1)} %bitcast.193, f32[256,16]{0,1:T(8,128)S(1)} %get-tuple-element.362, ...), kind=kOutput, calls=%fused_computation.29 | convolution fusion | flops 810287104 | bytes 3522560 | tf_op jit(solution)/shard_map/jvp()/while/body/eval_jaxpr/hij,jhp->ihp/dot_general | solution.py:37
  144.3 9.4 %all_to_all.93 = bf16[2,128,1024]{1,2,0:T(8,128)(2,1)S(1)} all-to-all(bf16[2,128,1024]{1,2,0:T(8,128)(2,1)S(1)} %copy.127), channel_id=1, replica_groups=mesh['seq'=2,'fsdp'=16] {'seq'}, dimensions={0} | all-to-all | bytes 1048576 | tf_op jit(solution)/shard_map/all_to_all | solution.py:162
  156.9 4.2 multiply_reduce_fusion.6
  161.2 2.8 fusion.41
  164.0 4.2 all-to-all-start.3
  170.5 2.7 mul.647
  173.3 3.2 convolution_bitcast_fusion
  181.1 5.8 fusion.7
  186.9 4.8 fusion.34
  191.7 2.7 copy.132
  198.1 3.2 convolution_bitcast_fusion.1
  210.5 4.6 fusion.110
  216.0 2.5 reduce-window.28
  219.5 3.2 all-to-all-start.5
  223.9 2.7 all-to-all-done.5
  226.6 3.5 all-to-all-start.4
  231.1 5.5 all-to-all-done.4
  236.7 9.2 %fusion.68 = f32[1024,4384]{1,0:T(8,128)} fusion(bf16[128,32]{0,1:T(8,128)(2,1)S(1)} %bitcast.211, bf16[128,256]{0,1:T(8,128)(2,1)S(1)} %copy.149, bf16[128,2048]{0,1:T(8,128)(2,1)S(1)} %bitcast.199, bf16[128,2048]{0,1:T(8,128)(2,1)S(1)} %copy-done.13, bf16[128,1024]{1,0:T(8,128)(2,1)S(1)} %copy-done.5, f32[1024]{0:T(1024)S(1)} %copy-done.24, ...), kind=kOutput, calls=%fused_computation.108 | convolution fusion | flops 1154252800 | bytes 19345920 | tf_op jit(solution)/shard_map/dot_general | solution.py:212
  246.6 4.2 fusion.33
  255.8 71.8 %reduce-scatter.8.cloned.1.call-done = f32[128,1024]{1,0:T(8,128)} async-done(((f32[2048,1024]{1,0:T(8,128)}), f32[128,1024]{1,0:T(8,128)}) %reduce-scatter.8.cloned.1.call-update) | async-done | bytes 524304 | tf_op jit(solution)/shard_map/reduce_scatter | solution.py:176
  327.5 193.4 %reduce-scatter.6.cloned.1.call-done = f32[64,4384]{1,0:T(8,128)} async-done(((f32[1024,4384]{1,0:T(8,128)}), f32[64,4384]{1,0:T(8,128)}) %reduce-scatter.6.cloned.1.call-update) | async-done | bytes 1122320 | tf_op jit(solution)/shard_map/reduce_scatter | solution.py:211
  521.9 6.8 %fusion.51 = (f32[1024]{0:T(1024)S(1)}, f32[128]{0:T(128)S(1)}, f32[128,1024]{1,0:T(8,128)S(1)}) fusion(bf16[128,1024]{1,0:T(8,128)(2,1)S(1)} %copy-done.5, f32[128]{0:T(128)S(1)} %copy-done.62, f32[1024]{0:T(1024)S(1)} %copy-done.24, bf16[1024,4384]{1,0:T(8,128)(2,1)} %all-gather.3.cloned.1.call-done, bf16[128,32]{0,1:T(8,128)(2,1)S(1)} %bitcast.212, ...), kind=kOutput, calls=%fused_computation.90 | convolution fusion | flops 1154644864 | bytes 10896384 | tf_op jit(solution)/shard_map/dot_general | solution.py:207
  528.7 59.6 %all-reduce.16 = (f32[4,2304]{1,0:T(4,128)S(1)}, f32[2304]{0:T(1024)S(1)}, f32[32]{0:T(128)S(1)}, f32[32]{0:T(128)S(1)}, f32[32]{0:T(128)S(1)}, /*index=5*/f32[1024]{0:T(1024)S(1)}, f32[2048]{0:T(1024)S(1)}) all-reduce(f32[4,2304]{1,0:T(4,128)S(1)} %add_dynamic-update-slice_fusion, ...), channel_id=1, replica_groups=mesh['seq'=2,'fsdp'=16] {'fsdp'}, use_global_device_ids=true, to_apply=%region_21.22 | all-reduce | flops 14688 | bytes 117504 | tf_op jit(solution)/shard_map/psum | solution.py:237
  588.3 9.4 %all-reduce.17 = (f32[4,2304]{1,0:T(4,128)}, f32[2304]{0:T(1024)}, f32[32]{0:T(128)}, f32[32]{0:T(128)}, f32[32]{0:T(128)}, /*index=5*/f32[1024]{0:T(1024)}, f32[2048]{0:T(1024)}) all-reduce(f32[4,2304]{1,0:T(4,128)S(1)} %get-tuple-element.320, f32[2304]{0:T(1024)S(1)} %get-tuple-element.321, ...), channel_id=1, replica_groups=mesh['seq'=2,'fsdp'=16] {'seq'}, use_global_device_ids=true, to_apply=%region_22.23 | all-reduce | flops 14688 | bytes 117504 | tf_op jit(solution)/shard_map/psum | solution.py:236
  (297 shorter events, 69.5 us)
Async XLA Ops:
  7.2 85.1 %copy-start.4 = (bf16[128,1024]{1,0:T(8,128)(2,1)S(1)}, bf16[128,1024]{1,0:T(8,128)(2,1)}, u32[]{:S(2)}) copy-start(bf16[128,1024]{1,0:T(8,128)(2,1)} %param.16) | copy-start | bytes 786436
  7.2 85.1 %copy-start.23 = (f32[1024]{0:T(1024)S(1)}, f32[1024]{0:T(1024)}, u32[]{:S(2)}) copy-start(f32[1024]{0:T(1024)} %param.25) | copy-start | bytes 12292
  7.2 85.1 %all-gather.3.cloned.1.call-start = ((), (), s32[]{:S(2)}) async-start(), calls=%async_computation.9 | async-start | bytes 9748480 | tf_op jit(solution)/shard_map/all_gather | solution.py:124
  7.9 149.0 %all-gather.5.cloned.1.call-start = ((), (), s32[]{:S(2)}) async-start(), calls=%async_computation.10 | async-start | bytes 4456448 | tf_op jit(solution)/shard_map/all_gather | solution.py:169
  11.6 101.8 %copy-start.78 = (f32[16]{0:T(128)}, f32[16]{0:T(128)S(1)}, u32[]{:S(2)}) copy-start(f32[16]{0:T(128)S(1)} %dynamic_slice.89) | copy-start | bytes 196
  14.3 107.2 %copy-start.31 = (f32[1280]{0:T(1024)}, f32[1280]{0:T(1024)S(1)}, u32[]{:S(2)}) copy-start(f32[1280]{0:T(1024)S(1)} %get-tuple-element.316) | copy-start | bytes 15364
  14.3 107.2 %copy-start.33 = (f32[1280]{0:T(1024)}, f32[1280]{0:T(1024)S(1)}, u32[]{:S(2)}) copy-start(f32[1280]{0:T(1024)S(1)} %get-tuple-element.318) | copy-start | bytes 15364
  14.3 107.2 %copy-start.35 = (f32[1280]{0:T(1024)}, f32[1280]{0:T(1024)S(1)}, u32[]{:S(2)}) copy-start(f32[1280]{0:T(1024)S(1)} %get-tuple-element.319) | copy-start | bytes 15364
  14.3 107.2 %copy-start.37 = (f32[1280]{0:T(1024)}, f32[1280]{0:T(1024)S(1)}, u32[]{:S(2)}) copy-start(f32[1280]{0:T(1024)S(1)} %get-tuple-element.317) | copy-start | bytes 15364
  15.1 98.2 %copy-start.80 = (f32[16]{0:T(128)}, f32[16]{0:T(128)S(1)}, u32[]{:S(2)}) copy-start(f32[16]{0:T(128)S(1)} %fusion.100) | copy-start | bytes 196
  16.0 105.5 %copy-start.76 = (f32[256]{0:T(256)}, f32[256]{0:T(256)S(1)}, u32[]{:S(2)}) copy-start(f32[256]{0:T(256)S(1)} %pad_convert_fusion.1) | copy-start | bytes 3076
  17.8 103.8 %copy-start.70 = (f32[256]{0:T(256)}, f32[256]{0:T(256)S(1)}, u32[]{:S(2)}) copy-start(f32[256]{0:T(256)S(1)} %get-tuple-element.371) | copy-start | bytes 3076
  17.8 103.8 %copy-start.72 = (f32[256]{0:T(256)}, f32[256]{0:T(256)S(1)}, u32[]{:S(2)}) copy-start(f32[256]{0:T(256)S(1)} %get-tuple-element.372) | copy-start | bytes 3076
  20.2 79.4 %copy-start.83 = (f32[128]{0:T(128)}, f32[128]{0:T(128)S(1)}, u32[]{:S(2)}) copy-start(f32[128]{0:T(128)S(1)} %fusion.53) | copy-start | bytes 1540
  20.2 79.4 %copy-start.61 = (f32[128]{0:T(128)}, f32[128]{0:T(128)S(1)}, u32[]{:S(2)}) copy-start(f32[128]{0:T(128)S(1)} %fusion.99) | copy-start | bytes 1540
  99.6 21.7 %copy-start.6 = (bf16[128,4384]{0,1:T(8,128)(2,1)}, bf16[128,4384]{0,1:T(8,128)(2,1)S(1)}, u32[]{:S(2)}) copy-start(bf16[128,4384]{0,1:T(8,128)(2,1)S(1)} %convolution_convert_fusion) | copy-start | bytes 3366916
  100.3 9.2 %all-to-all-start = ((bf16[128,2,16]{0,2,1:T(8,128)(2,1)}), bf16[128,2,16]{0,2,1:T(8,128)(2,1)S(1)}, u32[]{:S(2)}, u32[]{:S(2)}) async-start(bf16[128,2,16]{0,2,1:T(8,128)(2,1)} %bitcast.3), calls=%async_computation | async-start | bytes 16384 | tf_op jit(solution)/shard_map/all_to_all | solution.py:134
  109.5 11.6 %all-to-all-start.1 = ((bf16[128,2,1024]{0,2,1:T(8,128)(2,1)}), bf16[128,2,1024]{0,2,1:T(8,128)(2,1)S(1)}, u32[]{:S(2)}, u32[]{:S(2)}) async-start(bf16[128,2,1024]{0,2,1:T(8,128)(2,1)} %bitcast.6), calls=%async_computation.1 | async-start | bytes 1048576 | tf_op jit(solution)/shard_map/all_to_all | solution.py:133
  164.0 12.5 %all-to-all-start.3 = ((bf16[128,2,1024]{0,2,1:T(8,128)(2,1)}), bf16[128,2,1024]{0,2,1:T(8,128)(2,1)}, u32[]{:S(2)}, u32[]{:S(2)}) async-start(bf16[128,2,1024]{0,2,1:T(8,128)(2,1)} %bitcast.201), calls=%async_computation.3 | async-start | bytes 1048576 | tf_op jit(solution)/shard_map/all_to_all | solution.py:183
  168.2 61.9 %reduce-scatter.10.cloned.1.call-start = ((), (), s32[]{:S(2)}) async-start(), calls=%async_computation.13 | async-start | bytes 196608
  209.7 41.1 %copy-start.49 = (f32[1280]{0:T(1024)}, f32[1280]{0:T(1024)S(1)}, u32[]{:S(2)}) copy-start(f32[1280]{0:T(1024)S(1)} %get-tuple-element.312) | copy-start | bytes 15364
  210.4 117.1 %reduce-scatter.8.cloned.1.call-start = ((), (), s32[]{:S(2)}) async-start(), calls=%async_computation.12 | async-start | bytes 8912896 | tf_op jit(solution)/shard_map/reduce_scatter | solution.py:176
  219.5 7.0 %all-to-all-start.5 = ((bf16[2,128,16]{1,2,0:T(8,128)(2,1)}), bf16[2,128,16]{1,2,0:T(8,128)(2,1)S(1)}, u32[]{:S(2)}, u32[]{:S(2)}) async-start(bf16[2,128,16]{1,2,0:T(8,128)(2,1)} %copy_bitcast_fusion.3), calls=%async_computation.5 | async-start | bytes 16384 | tf_op jit(solution)/shard_map/all_to_all | solution.py:197
  222.8 13.8 %copy-start.5 = (bf16[128,1024]{1,0:T(8,128)(2,1)S(1)}, bf16[128,1024]{1,0:T(8,128)(2,1)}, u32[]{:S(2)}) copy-start(bf16[128,1024]{1,0:T(8,128)(2,1)} %param.16) | copy-start | bytes 786436
  222.8 13.8 %copy-start.13 = (bf16[128,2048]{0,1:T(8,128)(2,1)S(1)}, bf16[128,2048]{0,1:T(8,128)(2,1)}, u32[]{:S(2)}) copy-start(bf16[128,2048]{0,1:T(8,128)(2,1)} %get-tuple-element.349) | copy-start | bytes 1572868
  222.8 13.8 %copy-start.24 = (f32[1024]{0:T(1024)S(1)}, f32[1024]{0:T(1024)}, u32[]{:S(2)}) copy-start(f32[1024]{0:T(1024)} %param.25) | copy-start | bytes 12292
  226.6 10.1 %all-to-all-start.4 = ((bf16[2,128,1024]{1,2,0:T(8,128)(2,1)}), bf16[2,128,1024]{1,2,0:T(8,128)(2,1)S(1)}, u32[]{:S(2)}, u32[]{:S(2)}) async-start(bf16[2,128,1024]{1,2,0:T(8,128)(2,1)} %copy.133), calls=%async_computation.4 | async-start | bytes 1048576 | tf_op jit(solution)/shard_map/all_to_all | solution.py:190
  230.1 290.9 %reduce-scatter.6.cloned.1.call-start = ((), (), s32[]{:S(2)}) async-start(), calls=%async_computation.11 | async-start | bytes 19496960 | tf_op jit(solution)/shard_map/reduce_scatter | solution.py:211
  246.0 352.7 %all-reduce.21.cloned.1.call-start = ((), (), s32[]{:S(2)}) async-start(), calls=%async_computation.14 | async-start | bytes 3342336 | tf_op jit(solution)/shard_map/psum | solution.py:219
  254.7 266.3 %copy-start.89 = (f32[32]{0:T(128)S(1)}, f32[32]{0:T(128)}, u32[]{:S(2)}) copy-start(f32[32]{0:T(128)} %param.23) | copy-start | bytes 388
  254.8 267.1 %copy-start.15 = (bf16[2,128,1024]{1,2,0:T(8,128)(2,1)S(1)}, bf16[2,128,1024]{1,2,0:T(8,128)(2,1)}, u32[]{:S(2)}) copy-start(bf16[2,128,1024]{1,2,0:T(8,128)(2,1)} %copy-done.14) | copy-start | bytes 1572868
  521.9 75.8 %copy-start.84 = (f32[128]{0:T(128)S(1)}, f32[128]{0:T(128)}, u32[]{:S(2)}) copy-start(f32[128]{0:T(128)} %copy-done.83) | copy-start | bytes 1540
  (69 other events, 254.7 us)
Sparse Core Ops, SparseCore 0:
  10.3 81.9 all-gather.2
  94.5 48.8 all-gather.4
  210.5 9.5 reduce-scatter.9
  224.0 103.4 reduce-scatter.7
  331.6 189.3 reduce-scatter.5
  523.2 52.7 all-reduce.20
